TPU v7x, 512 devices: a whole 4x8x8 slice. The times are simulated.
512 devices in a mesh: tm: 256 (over z, y, x), state: 2 (over core).
Axes of the slice: x: 4, y: 8, z: 8, core: 2. Of those that a mesh axis runs over, the one named last changes fastest.
Arguments:
- features: float32 [4, 4096, 512], P(None, 'tm'), may hold values from -18 to 18
- gauss_means: float32 [1024, 512], P('state'), may hold values from -3 to 3
- precisions: float32 [1024, 512], P('state'), may hold values from 0.5 to 2
- transitions: bfloat16 [1024, 1024], P('state'), may hold values from 0 to 1, as said below
- initial: bfloat16 [1024], P('state'), may hold values from 0.099609375 to 10
- reset_flags: int32 [4, 4096], P(None, 'tm'), may hold values from 0 to 1, as said below
Outputs:
- posteriors: bfloat16 [4, 4096, 1024], P(None, 'tm', 'state')
- evidence: float32 [4, 4096], P(None, ('tm', 'state'))
Inputs may be any that keep to these rules, and one draw needn't show every extreme that they name: `transitions`: every entry nonnegative; each row sums to 1 up to the rounding of its entries; the diagonal holds half or more of each row. reset_flags[b, 0] = 1 in every stream; the runs of frames from one 1 to the next (utterances) hold 1 to 16 frames, and some hold exactly 16.
All inputs are finite; a program needn't handle non-finite values.
Results may differ from a plain program's by a relative error of at most 0.012.
Values may be sent and summed in bfloat16 or wider, within the bound.
No kernel may reach another device: no remote copies, remote signals or barrier semaphores. Data moves between devices by JAX's collectives and lax.ppermute only.
A program may use at most 64 MiB of HBM per device.

v0:
```python
import jax
import jax.numpy as jnp
from jax import lax
from jax.sharding import PartitionSpec as P

SPAN = 1
acoustic = 0.1


def in_one_piece(arrays, axis, dim, along):
    columns = [a.reshape(*a.shape[:along], -1) for a in arrays]
    both = jnp.concatenate(columns, axis=along)
    out, at, gathered = (lax.all_gather(both, axis, axis=dim, tiled=True), 0, [])
    for a, column in zip(arrays, columns):
        piece = out[..., at : at + column.shape[along]]
        gathered.append(piece.reshape(*piece.shape[:along], *a.shape[along:]))
        at += column.shape[along]
    return tuple(gathered)


def passed_along(block, axis, distance):
    devices = range(lax.axis_size(axis))
    route = [(i - distance, i) for i in devices if i - distance in devices]
    return lax.ppermute(block, axis, route)


def local_scores(features, gauss_means, precisions):
    streams, frames, feat_width = features.shape
    highest = lax.Precision.HIGHEST
    flat_feats = features.reshape(streams * frames, feat_width)
    quadratic = jnp.dot(flat_feats * flat_feats, (-0.5 * precisions).T, precision=highest)
    linear_part = jnp.dot(flat_feats, (precisions * gauss_means).T, precision=highest)
    offset = 0.5 * jnp.sum(jnp.log(precisions) - precisions * gauss_means * gauss_means, axis=1)
    return (acoustic * (quadratic + linear_part + offset)).reshape(
        streams, frames, gauss_means.shape[0]
    )


def run_block(emission_t, reset_t, trans, trans_back, prior_dist, alpha_in, beta_in):
    states = trans.shape[0]

    def forward_step(alpha_prev, inputs):
        emit_row, reset_row = inputs
        predicted = jnp.dot(
            alpha_prev.astype(jnp.bfloat16), trans, preferred_element_type=jnp.float32
        )
        predicted = jnp.where(reset_row[:, None] == 1, prior_dist[None, :], predicted)
        weighted = emit_row * predicted
        norm_total = jnp.sum(weighted, axis=1)
        alpha_next = weighted / norm_total[:, None]
        return (alpha_next, (alpha_next, jnp.log(norm_total)))

    alpha_out, (alphas, log_norms) = lax.scan(forward_step, alpha_in, (emission_t, reset_t))

    def backward_step(beta_next, inputs):
        emit_row, reset_row = inputs
        spread = jnp.dot(
            (emit_row * beta_next).astype(jnp.bfloat16),
            trans_back,
            preferred_element_type=jnp.float32,
        )
        spread = spread / jnp.sum(spread, axis=1, keepdims=True)
        beta_prev = jnp.where(reset_row[:, None] == 1, 1.0 / states, spread)
        return (beta_prev, beta_next)

    beta_out, betas = lax.scan(backward_step, beta_in, (emission_t, reset_t), reverse=True)
    return (alpha_out, alphas, log_norms, beta_out, betas)


def run_chain(scores, resets, trans, trans_back, prior_dist, relay_step, relays):
    maxima = jnp.max(scores, axis=2, keepdims=True)
    emission_t = jnp.swapaxes(jnp.exp(scores - maxima), 0, 1)
    reset_t = jnp.swapaxes(resets, 0, 1)
    streams, states = (scores.shape[0], scores.shape[2])
    alpha_in = jnp.full((streams, states), 1.0 / states, jnp.float32)
    beta_in = alpha_in
    for relay_turn in range(relays + 1):
        alpha_out, alphas, log_norms, beta_out, betas = run_block(
            emission_t, reset_t, trans, trans_back, prior_dist, alpha_in, beta_in
        )
        if relay_turn < relays:
            alpha_in, beta_in = relay_step(alpha_out, beta_out)
    product = alphas * betas
    posterior = (product / jnp.sum(product, axis=2, keepdims=True)).astype(jnp.bfloat16)
    return (jnp.swapaxes(posterior, 0, 1), jnp.swapaxes(log_norms, 0, 1))


def per_device(features, gauss_means, precisions, transitions, initial, reset_flags):
    trans, prior_raw = in_one_piece((transitions, initial), "state", 0, 1)
    trans_back = trans.T
    states = trans.shape[0]
    prior_float = prior_raw.astype(jnp.float32)
    prior_dist = prior_float / jnp.sum(prior_float)
    scores = local_scores(features, gauss_means, precisions)
    group = lax.axis_size("state")
    place = lax.axis_index("state")
    blocks = lax.axis_size("tm")
    block_place = lax.axis_index("tm")
    quarter = features.shape[1] // group
    is_last = block_place * group + place == blocks * group - 1

    def relay_step(alpha_out, beta_out):
        alpha_next = passed_along(alpha_out, ("tm", "state"), 1)
        beta_next = passed_along(beta_out, ("tm", "state"), -1)
        beta_next = jnp.where(is_last, 1.0 / states, beta_next)
        return (alpha_next, beta_next)

    my_scores = lax.all_to_all(scores, "state", split_axis=1, concat_axis=2, tiled=True)
    my_flags = lax.dynamic_slice_in_dim(reset_flags, place * quarter, quarter, 1)
    posterior, evidence = run_chain(
        my_scores, my_flags, trans, trans_back, prior_dist, relay_step, SPAN * group
    )
    posteriors = lax.all_to_all(posterior, "state", split_axis=2, concat_axis=1, tiled=True)
    return (posteriors, evidence)


def solution(mesh):
    return jax.shard_map(
        per_device,
        mesh=mesh,
        in_specs=(
            P(None, "tm", None),
            P("state", None),
            P("state", None),
            P("state", None),
            P("state"),
            P(None, "tm"),
        ),
        out_specs=(P(None, "tm", "state"), P(None, ("tm", "state"))),
        check_vma=False,
    )
```

profile of v0, /device:TPU:257, one launch (start us, length us, event | category | flops | bytes accessed | tf_op | source)
XLA Modules:
  0.0 149.7 jit_solution(1743918318548357542)
XLA Ops:
  7.2 1.5 %copy.41 = bf16[512,1024]{0,1:T(8,128)(2,1)S(1)} copy(bf16[512,1024]{1,0:T(8,128)(2,1)} %param.21) | data formatting | bytes 2097152 | tf_op args[3]
  8.8 1.1 pad_maximum_fusion
  11.0 1.1 fusion.30
  12.0 1.2 fusion.27
  13.2 0.7 copy.38
  14.0 4.0 %all-to-all-start = ((f32[4,16,512]{2,0,1:T(4,128)}), f32[4,16,512]{2,0,1:T(4,128)S(1)}, u32[]{:S(2)}, u32[]{:S(2)}) async-start(f32[4,16,512]{2,0,1:T(4,128)} %copy.38), calls=%async_computation | async-start | bytes 262144 | tf_op jit(solution)/shard_map/all_to_all | solution.py:108
  18.2 0.9 all-to-all-done
  19.4 11.7 %all-gather.2.cloned.1.call-done = bf16[1024,1025]{0,1:T(8,128)(2,1)} async-done(((bf16[512,1025]{0,1:T(8,128)(2,1)}), bf16[1024,1025]{0,1:T(8,128)(2,1)}) %all-gather.2.cloned.1.call-update) | async-done | bytes 2099216 | tf_op jit(solution)/shard_map/all_gather | solution.py:13
  31.1 3.5 %slice_bitcast_fusion = (bf16[1024,1024]{1,0:T(8,128)(2,1)S(1)}, bf16[1024,1024]{0,1:T(8,128)(2,1)}) fusion(bf16[1024,1025]{0,1:T(8,128)(2,1)} %all-gather.2.cloned.1.call-done), kind=kLoop, calls=%fused_computation.68 | loop fusion | bytes 6291456 | tf_op jit(solution)/shard_map/transpose | solution.py:90
  34.6 3.9 %copy.42 = bf16[1024,1024]{1,0:T(8,128)(2,1)} copy(bf16[1024,1024]{0,1:T(8,128)(2,1)} %get-tuple-element.648) | data formatting | bytes 4194304
  38.5 1.4 fusion.37
  39.9 1.3 fusion.36
  41.2 17.6 %while.84 = (s32[]{:T(128)}, f32[4,1024]{1,0:T(4,128)S(1)}, f32[8,4,1024]{2,1,0:T(4,128)S(1)}, s32[8,4]{1,0:T(8,128)S(1)}, f32[1024]{0:T(1024)S(1)}, /*index=5*/bf16[1024,1024]{1,0:T(8,128)(2,1)}, s32[]{:T(128)}, s32[]{:T(128)}) while((s32[]{:T(128)}, f32[4,1024]{1,0:T(4,128)S(1)}, f32[8,4,1024]{2,1,0:T(4,128)S(1)}, ...), condition=%wide.region_5.6_spmd.clone, body=%wide.region_3.5_spmd.clone.sunk | while | flops 8409091 | bytes 2183327 | solution.py:53
  41.2 2.1 %fusion.76 = (f32[4]{0:T(128)S(1)}, f32[4,1024]{1,0:T(4,128)S(1)}) fusion(bf16[1024,1024]{1,0:T(8,128)(2,1)} %get-tuple-element.916, f32[4,1024]{1,0:T(4,128)S(1)} %get-tuple-element.904, pred[]{:T(512)S(6)} %compare.6, f32[1024]{0:T(1024)S(1)} %get-tuple-element.915, pred[4]{0:T(512)(128)(4,1)S(1)} %compare_bitcast_fusion.16, ...), kind=kOutput, calls=%fused_computation.73.clone.1 | convolution fusion | flops 8404988 | bytes 2150425 | tf_op jit(solution)/shard_map/while/body/eval_jaxpr/dot_general | solution.py:44
  43.4 2.1 %fusion.76 = (f32[4]{0:T(128)S(1)}, f32[4,1024]{1,0:T(4,128)S(1)}) fusion(bf16[1024,1024]{1,0:T(8,128)(2,1)} %get-tuple-element.916, f32[4,1024]{1,0:T(4,128)S(1)} %get-tuple-element.904, pred[]{:T(512)S(6)} %compare.6, f32[1024]{0:T(1024)S(1)} %get-tuple-element.915, pred[4]{0:T(512)(128)(4,1)S(1)} %compare_bitcast_fusion.16, ...), kind=kOutput, calls=%fused_computation.73.clone.1 | convolution fusion | flops 8404988 | bytes 2150425 | tf_op jit(solution)/shard_map/while/body/eval_jaxpr/dot_general | solution.py:44
  45.6 2.1 %fusion.76 = (f32[4]{0:T(128)S(1)}, f32[4,1024]{1,0:T(4,128)S(1)}) fusion(bf16[1024,1024]{1,0:T(8,128)(2,1)} %get-tuple-element.916, f32[4,1024]{1,0:T(4,128)S(1)} %get-tuple-element.904, pred[]{:T(512)S(6)} %compare.6, f32[1024]{0:T(1024)S(1)} %get-tuple-element.915, pred[4]{0:T(512)(128)(4,1)S(1)} %compare_bitcast_fusion.16, ...), kind=kOutput, calls=%fused_computation.73.clone.1 | convolution fusion | flops 8404988 | bytes 2150425 | tf_op jit(solution)/shard_map/while/body/eval_jaxpr/dot_general | solution.py:44
  47.8 2.1 %fusion.76 = (f32[4]{0:T(128)S(1)}, f32[4,1024]{1,0:T(4,128)S(1)}) fusion(bf16[1024,1024]{1,0:T(8,128)(2,1)} %get-tuple-element.916, f32[4,1024]{1,0:T(4,128)S(1)} %get-tuple-element.904, pred[]{:T(512)S(6)} %compare.6, f32[1024]{0:T(1024)S(1)} %get-tuple-element.915, pred[4]{0:T(512)(128)(4,1)S(1)} %compare_bitcast_fusion.16, ...), kind=kOutput, calls=%fused_computation.73.clone.1 | convolution fusion | flops 8404988 | bytes 2150425 | tf_op jit(solution)/shard_map/while/body/eval_jaxpr/dot_general | solution.py:44
  50.0 2.1 %fusion.76 = (f32[4]{0:T(128)S(1)}, f32[4,1024]{1,0:T(4,128)S(1)}) fusion(bf16[1024,1024]{1,0:T(8,128)(2,1)} %get-tuple-element.916, f32[4,1024]{1,0:T(4,128)S(1)} %get-tuple-element.904, pred[]{:T(512)S(6)} %compare.6, f32[1024]{0:T(1024)S(1)} %get-tuple-element.915, pred[4]{0:T(512)(128)(4,1)S(1)} %compare_bitcast_fusion.16, ...), kind=kOutput, calls=%fused_computation.73.clone.1 | convolution fusion | flops 8404988 | bytes 2150425 | tf_op jit(solution)/shard_map/while/body/eval_jaxpr/dot_general | solution.py:44
  52.2 2.1 %fusion.76 = (f32[4]{0:T(128)S(1)}, f32[4,1024]{1,0:T(4,128)S(1)}) fusion(bf16[1024,1024]{1,0:T(8,128)(2,1)} %get-tuple-element.916, f32[4,1024]{1,0:T(4,128)S(1)} %get-tuple-element.904, pred[]{:T(512)S(6)} %compare.6, f32[1024]{0:T(1024)S(1)} %get-tuple-element.915, pred[4]{0:T(512)(128)(4,1)S(1)} %compare_bitcast_fusion.16, ...), kind=kOutput, calls=%fused_computation.73.clone.1 | convolution fusion | flops 8404988 | bytes 2150425 | tf_op jit(solution)/shard_map/while/body/eval_jaxpr/dot_general | solution.py:44
  54.4 2.1 %fusion.76 = (f32[4]{0:T(128)S(1)}, f32[4,1024]{1,0:T(4,128)S(1)}) fusion(bf16[1024,1024]{1,0:T(8,128)(2,1)} %get-tuple-element.916, f32[4,1024]{1,0:T(4,128)S(1)} %get-tuple-element.904, pred[]{:T(512)S(6)} %compare.6, f32[1024]{0:T(1024)S(1)} %get-tuple-element.915, pred[4]{0:T(512)(128)(4,1)S(1)} %compare_bitcast_fusion.16, ...), kind=kOutput, calls=%fused_computation.73.clone.1 | convolution fusion | flops 8404988 | bytes 2150425 | tf_op jit(solution)/shard_map/while/body/eval_jaxpr/dot_general | solution.py:44
  56.6 2.1 %fusion.76 = (f32[4]{0:T(128)S(1)}, f32[4,1024]{1,0:T(4,128)S(1)}) fusion(bf16[1024,1024]{1,0:T(8,128)(2,1)} %get-tuple-element.916, f32[4,1024]{1,0:T(4,128)S(1)} %get-tuple-element.904, pred[]{:T(512)S(6)} %compare.6, f32[1024]{0:T(1024)S(1)} %get-tuple-element.915, pred[4]{0:T(512)(128)(4,1)S(1)} %compare_bitcast_fusion.16, ...), kind=kOutput, calls=%fused_computation.73.clone.1 | convolution fusion | flops 8404988 | bytes 2150425 | tf_op jit(solution)/shard_map/while/body/eval_jaxpr/dot_general | solution.py:44
  58.8 3.2 %collective-permute-start = (f32[4,1024]{1,0:T(4,128)S(1)}, f32[4,1024]{1,0:T(4,128)S(1)}, u32[]{:S(2)}, u32[]{:S(2)}) collective-permute-start(f32[4,1024]{1,0:T(4,128)S(1)} %get-tuple-element.437), channel_id=1, source_target_pairs={{0,1},{1,2},{2,3},{3,4},{4,5},{5,6},{6,7},{7,8},{8,9},{9,10},{10,1... | collective-permute-start | bytes 49160 | tf_op jit(solution)/shard_map/ppermute | solution.py:24
  62.0 4.8 %while.85 = (s32[]{:T(128)}, f32[4,1024]{1,0:T(4,128)S(1)}, s32[8,4]{1,0:T(8,128)S(1)}, f32[8,4,1024]{2,1,0:T(4,128)S(1)}, bf16[1024,1024]{1,0:T(8,128)(2,1)S(1)}, /*index=5*/s32[]{:T(128)}, s32[]{:T(128)}, s32[]{:T(128)}) while((s32[]{:T(128)}, f32[4,1024]{1,0:T(4,128)S(1)}, s32[8,4]{1,0:T(8,128)S(1)}, ...), condition=%wide.region_14.15_spmd.clone, body=%wide.region_12.14_spmd.clone.sunk | while | flops 8413188 | bytes 2179243 | solution.py:66
  63.2 0.5 fusion.78
  65.0 0.5 fusion.78
  66.2 0.5 fusion.78
  66.8 1.9 %collective-permute-start.2 = (f32[4,1024]{1,0:T(4,128)S(1)}, f32[4,1024]{1,0:T(4,128)S(1)}, u32[]{:S(2)}, u32[]{:S(2)}) collective-permute-start(f32[4,1024]{1,0:T(4,128)S(1)} %get-tuple-element.440), channel_id=1, source_target_pairs={{1,0},{2,1},{3,2},{4,3},{5,4},{6,5},{7,6},{8,7},{9,8},{10,9},{11,1... | collective-permute-start | bytes 49160 | tf_op jit(solution)/shard_map/ppermute | solution.py:24
  68.7 17.6 %while.80 = (s32[]{:T(128)}, f32[4,1024]{1,0:T(4,128)S(1)}, f32[8,4,1024]{2,1,0:T(4,128)S(1)}, s32[8,4]{1,0:T(8,128)S(1)}, f32[1024]{0:T(1024)S(1)}, /*index=5*/bf16[1024,1024]{1,0:T(8,128)(2,1)}, s32[]{:T(128)}) while((s32[]{:T(128)}, f32[4,1024]{1,0:T(4,128)S(1)}, f32[8,4,1024]{2,1,0:T(4,128)S(1)}, s32[8,4]{1,0:T(8,128)S(1)}, ...), condition=%wide.region_8.9_spmd, body=%wide.region_6.8_spmd.sunk | while | flops 8409090 | bytes 2183309 | solution.py:53
  68.7 2.1 %fusion.67 = (f32[4]{0:T(128)S(1)}, f32[4,1024]{1,0:T(4,128)S(1)}) fusion(bf16[1024,1024]{1,0:T(8,128)(2,1)} %get-tuple-element.938, f32[4,1024]{1,0:T(4,128)S(1)} %get-tuple-element.927, f32[1024]{0:T(1024)S(1)} %get-tuple-element.937, pred[4]{0:T(512)(128)(4,1)S(1)} %compare_bitcast_fusion.12, f32[8,4,1024]{2,1,0:T(4,128)S(1)} %get-tuple-element.935, ...), kind=kOutput, calls=%fused_computation.69.clone.1 | convolution fusion | flops 8404988 | bytes 2150424 | tf_op jit(solution)/shard_map/while/body/eval_jaxpr/dot_general | solution.py:44
  70.9 2.1 %fusion.67 = (f32[4]{0:T(128)S(1)}, f32[4,1024]{1,0:T(4,128)S(1)}) fusion(bf16[1024,1024]{1,0:T(8,128)(2,1)} %get-tuple-element.938, f32[4,1024]{1,0:T(4,128)S(1)} %get-tuple-element.927, f32[1024]{0:T(1024)S(1)} %get-tuple-element.937, pred[4]{0:T(512)(128)(4,1)S(1)} %compare_bitcast_fusion.12, f32[8,4,1024]{2,1,0:T(4,128)S(1)} %get-tuple-element.935, ...), kind=kOutput, calls=%fused_computation.69.clone.1 | convolution fusion | flops 8404988 | bytes 2150424 | tf_op jit(solution)/shard_map/while/body/eval_jaxpr/dot_general | solution.py:44
  73.1 2.1 %fusion.67 = (f32[4]{0:T(128)S(1)}, f32[4,1024]{1,0:T(4,128)S(1)}) fusion(bf16[1024,1024]{1,0:T(8,128)(2,1)} %get-tuple-element.938, f32[4,1024]{1,0:T(4,128)S(1)} %get-tuple-element.927, f32[1024]{0:T(1024)S(1)} %get-tuple-element.937, pred[4]{0:T(512)(128)(4,1)S(1)} %compare_bitcast_fusion.12, f32[8,4,1024]{2,1,0:T(4,128)S(1)} %get-tuple-element.935, ...), kind=kOutput, calls=%fused_computation.69.clone.1 | convolution fusion | flops 8404988 | bytes 2150424 | tf_op jit(solution)/shard_map/while/body/eval_jaxpr/dot_general | solution.py:44
  75.3 2.1 %fusion.67 = (f32[4]{0:T(128)S(1)}, f32[4,1024]{1,0:T(4,128)S(1)}) fusion(bf16[1024,1024]{1,0:T(8,128)(2,1)} %get-tuple-element.938, f32[4,1024]{1,0:T(4,128)S(1)} %get-tuple-element.927, f32[1024]{0:T(1024)S(1)} %get-tuple-element.937, pred[4]{0:T(512)(128)(4,1)S(1)} %compare_bitcast_fusion.12, f32[8,4,1024]{2,1,0:T(4,128)S(1)} %get-tuple-element.935, ...), kind=kOutput, calls=%fused_computation.69.clone.1 | convolution fusion | flops 8404988 | bytes 2150424 | tf_op jit(solution)/shard_map/while/body/eval_jaxpr/dot_general | solution.py:44
  77.5 2.1 %fusion.67 = (f32[4]{0:T(128)S(1)}, f32[4,1024]{1,0:T(4,128)S(1)}) fusion(bf16[1024,1024]{1,0:T(8,128)(2,1)} %get-tuple-element.938, f32[4,1024]{1,0:T(4,128)S(1)} %get-tuple-element.927, f32[1024]{0:T(1024)S(1)} %get-tuple-element.937, pred[4]{0:T(512)(128)(4,1)S(1)} %compare_bitcast_fusion.12, f32[8,4,1024]{2,1,0:T(4,128)S(1)} %get-tuple-element.935, ...), kind=kOutput, calls=%fused_computation.69.clone.1 | convolution fusion | flops 8404988 | bytes 2150424 | tf_op jit(solution)/shard_map/while/body/eval_jaxpr/dot_general | solution.py:44
  79.7 2.1 %fusion.67 = (f32[4]{0:T(128)S(1)}, f32[4,1024]{1,0:T(4,128)S(1)}) fusion(bf16[1024,1024]{1,0:T(8,128)(2,1)} %get-tuple-element.938, f32[4,1024]{1,0:T(4,128)S(1)} %get-tuple-element.927, f32[1024]{0:T(1024)S(1)} %get-tuple-element.937, pred[4]{0:T(512)(128)(4,1)S(1)} %compare_bitcast_fusion.12, f32[8,4,1024]{2,1,0:T(4,128)S(1)} %get-tuple-element.935, ...), kind=kOutput, calls=%fused_computation.69.clone.1 | convolution fusion | flops 8404988 | bytes 2150424 | tf_op jit(solution)/shard_map/while/body/eval_jaxpr/dot_general | solution.py:44
  81.9 2.1 %fusion.67 = (f32[4]{0:T(128)S(1)}, f32[4,1024]{1,0:T(4,128)S(1)}) fusion(bf16[1024,1024]{1,0:T(8,128)(2,1)} %get-tuple-element.938, f32[4,1024]{1,0:T(4,128)S(1)} %get-tuple-element.927, f32[1024]{0:T(1024)S(1)} %get-tuple-element.937, pred[4]{0:T(512)(128)(4,1)S(1)} %compare_bitcast_fusion.12, f32[8,4,1024]{2,1,0:T(4,128)S(1)} %get-tuple-element.935, ...), kind=kOutput, calls=%fused_computation.69.clone.1 | convolution fusion | flops 8404988 | bytes 2150424 | tf_op jit(solution)/shard_map/while/body/eval_jaxpr/dot_general | solution.py:44
  84.1 2.1 %fusion.67 = (f32[4]{0:T(128)S(1)}, f32[4,1024]{1,0:T(4,128)S(1)}) fusion(bf16[1024,1024]{1,0:T(8,128)(2,1)} %get-tuple-element.938, f32[4,1024]{1,0:T(4,128)S(1)} %get-tuple-element.927, f32[1024]{0:T(1024)S(1)} %get-tuple-element.937, pred[4]{0:T(512)(128)(4,1)S(1)} %compare_bitcast_fusion.12, f32[8,4,1024]{2,1,0:T(4,128)S(1)} %get-tuple-element.935, ...), kind=kOutput, calls=%fused_computation.69.clone.1 | convolution fusion | flops 8404988 | bytes 2150424 | tf_op jit(solution)/shard_map/while/body/eval_jaxpr/dot_general | solution.py:44
  86.3 3.6 %collective-permute-start.1 = (f32[4,1024]{1,0:T(4,128)S(1)}, f32[4,1024]{1,0:T(4,128)S(1)}, u32[]{:S(2)}, u32[]{:S(2)}) collective-permute-start(f32[4,1024]{1,0:T(4,128)S(1)} %get-tuple-element.438), channel_id=1, source_target_pairs={{0,1},{1,2},{2,3},{3,4},{4,5},{5,6},{6,7},{7,8},{8,9},{9,10},{10,1... | collective-permute-start | bytes 49160 | tf_op jit(solution)/shard_map/ppermute | solution.py:24
  90.0 4.8 %while.82 = (s32[]{:T(128)}, f32[4,1024]{1,0:T(4,128)S(1)}, s32[8,4]{1,0:T(8,128)S(1)}, f32[8,4,1024]{2,1,0:T(4,128)S(1)}, bf16[1024,1024]{1,0:T(8,128)(2,1)S(1)}, /*index=5*/s32[]{:T(128)}, s32[]{:T(128)}) while((s32[]{:T(128)}, f32[4,1024]{1,0:T(4,128)S(1)}, s32[8,4]{1,0:T(8,128)S(1)}, f32[8,4,1024]{2,1,0:T(4,128)S(1)}, ...), condition=%wide.region_17.18_spmd, body=%wide.region_15.17_spmd.sunk | while | flops 8409091 | bytes 2179225 | solution.py:66
  90.0 0.5 fusion.72
  90.6 0.5 fusion.72
  91.2 0.5 fusion.72
  91.7 0.5 fusion.72
  92.3 0.5 fusion.72
  92.9 0.5 fusion.72
  93.5 0.5 fusion.72
  94.1 0.5 fusion.72
  94.7 6.3 %collective-permute-start.3 = (f32[4,1024]{1,0:T(4,128)S(1)}, f32[4,1024]{1,0:T(4,128)S(1)}, u32[]{:S(2)}, u32[]{:S(2)}) collective-permute-start(f32[4,1024]{1,0:T(4,128)S(1)} %get-tuple-element.441), channel_id=1, source_target_pairs={{1,0},{2,1},{3,2},{4,3},{5,4},{6,5},{7,6},{8,7},{9,8},{10,9},{11,1... | collective-permute-start | bytes 49160 | tf_op jit(solution)/shard_map/ppermute | solution.py:24
  101.0 20.0 %while.81 = (s32[]{:T(128)}, f32[4,1024]{1,0:T(4,128)S(1)}, f32[8,4,1024]{2,0,1:T(8,128)S(1)}, f32[8,4]{1,0:T(8,128)S(1)}, f32[8,4,1024]{2,1,0:T(4,128)S(1)}, /*...) while((s32[]{:T(128)}, f32[4,1024]{1,0:T(4,128)S(1)}, ...), condition=%wide.region_11.12_spmd, body=%wide.region_9.11_spmd.sunk | while | flops 8413186 | bytes 2281725 | solution.py:53
  101.1 2.1 %fusion.69 = (f32[4]{0:T(128)S(1)}, f32[4,1024]{1,0:T(4,128)S(1)}) fusion(bf16[1024,1024]{1,0:T(8,128)(2,1)} %get-tuple-element.967, f32[4,1024]{1,0:T(4,128)S(1)} %get-tuple-element.951, f32[1024]{0:T(1024)S(1)} %get-tuple-element.966, pred[4]{0:T(512)(128)(4,1)S(1)} %compare_bitcast_fusion.13, f32[8,4,1024]{2,1,0:T(4,128)S(1)} %get-tuple-element.964, ...), kind=kOutput, calls=%fused_computation.70.clone.1 | convolution fusion | flops 8404988 | bytes 2150424 | tf_op jit(solution)/shard_map/while/body/eval_jaxpr/dot_general | solution.py:44
  103.6 2.1 %fusion.69 = (f32[4]{0:T(128)S(1)}, f32[4,1024]{1,0:T(4,128)S(1)}) fusion(bf16[1024,1024]{1,0:T(8,128)(2,1)} %get-tuple-element.967, f32[4,1024]{1,0:T(4,128)S(1)} %get-tuple-element.951, f32[1024]{0:T(1024)S(1)} %get-tuple-element.966, pred[4]{0:T(512)(128)(4,1)S(1)} %compare_bitcast_fusion.13, f32[8,4,1024]{2,1,0:T(4,128)S(1)} %get-tuple-element.964, ...), kind=kOutput, calls=%fused_computation.70.clone.1 | convolution fusion | flops 8404988 | bytes 2150424 | tf_op jit(solution)/shard_map/while/body/eval_jaxpr/dot_general | solution.py:44
  106.1 2.1 %fusion.69 = (f32[4]{0:T(128)S(1)}, f32[4,1024]{1,0:T(4,128)S(1)}) fusion(bf16[1024,1024]{1,0:T(8,128)(2,1)} %get-tuple-element.967, f32[4,1024]{1,0:T(4,128)S(1)} %get-tuple-element.951, f32[1024]{0:T(1024)S(1)} %get-tuple-element.966, pred[4]{0:T(512)(128)(4,1)S(1)} %compare_bitcast_fusion.13, f32[8,4,1024]{2,1,0:T(4,128)S(1)} %get-tuple-element.964, ...), kind=kOutput, calls=%fused_computation.70.clone.1 | convolution fusion | flops 8404988 | bytes 2150424 | tf_op jit(solution)/shard_map/while/body/eval_jaxpr/dot_general | solution.py:44
  108.6 2.1 %fusion.69 = (f32[4]{0:T(128)S(1)}, f32[4,1024]{1,0:T(4,128)S(1)}) fusion(bf16[1024,1024]{1,0:T(8,128)(2,1)} %get-tuple-element.967, f32[4,1024]{1,0:T(4,128)S(1)} %get-tuple-element.951, f32[1024]{0:T(1024)S(1)} %get-tuple-element.966, pred[4]{0:T(512)(128)(4,1)S(1)} %compare_bitcast_fusion.13, f32[8,4,1024]{2,1,0:T(4,128)S(1)} %get-tuple-element.964, ...), kind=kOutput, calls=%fused_computation.70.clone.1 | convolution fusion | flops 8404988 | bytes 2150424 | tf_op jit(solution)/shard_map/while/body/eval_jaxpr/dot_general | solution.py:44
  111.1 2.1 %fusion.69 = (f32[4]{0:T(128)S(1)}, f32[4,1024]{1,0:T(4,128)S(1)}) fusion(bf16[1024,1024]{1,0:T(8,128)(2,1)} %get-tuple-element.967, f32[4,1024]{1,0:T(4,128)S(1)} %get-tuple-element.951, f32[1024]{0:T(1024)S(1)} %get-tuple-element.966, pred[4]{0:T(512)(128)(4,1)S(1)} %compare_bitcast_fusion.13, f32[8,4,1024]{2,1,0:T(4,128)S(1)} %get-tuple-element.964, ...), kind=kOutput, calls=%fused_computation.70.clone.1 | convolution fusion | flops 8404988 | bytes 2150424 | tf_op jit(solution)/shard_map/while/body/eval_jaxpr/dot_general | solution.py:44
  113.6 2.1 %fusion.69 = (f32[4]{0:T(128)S(1)}, f32[4,1024]{1,0:T(4,128)S(1)}) fusion(bf16[1024,1024]{1,0:T(8,128)(2,1)} %get-tuple-element.967, f32[4,1024]{1,0:T(4,128)S(1)} %get-tuple-element.951, f32[1024]{0:T(1024)S(1)} %get-tuple-element.966, pred[4]{0:T(512)(128)(4,1)S(1)} %compare_bitcast_fusion.13, f32[8,4,1024]{2,1,0:T(4,128)S(1)} %get-tuple-element.964, ...), kind=kOutput, calls=%fused_computation.70.clone.1 | convolution fusion | flops 8404988 | bytes 2150424 | tf_op jit(solution)/shard_map/while/body/eval_jaxpr/dot_general | solution.py:44
  116.0 2.1 %fusion.69 = (f32[4]{0:T(128)S(1)}, f32[4,1024]{1,0:T(4,128)S(1)}) fusion(bf16[1024,1024]{1,0:T(8,128)(2,1)} %get-tuple-element.967, f32[4,1024]{1,0:T(4,128)S(1)} %get-tuple-element.951, f32[1024]{0:T(1024)S(1)} %get-tuple-element.966, pred[4]{0:T(512)(128)(4,1)S(1)} %compare_bitcast_fusion.13, f32[8,4,1024]{2,1,0:T(4,128)S(1)} %get-tuple-element.964, ...), kind=kOutput, calls=%fused_computation.70.clone.1 | convolution fusion | flops 8404988 | bytes 2150424 | tf_op jit(solution)/shard_map/while/body/eval_jaxpr/dot_general | solution.py:44
  118.5 2.1 %fusion.69 = (f32[4]{0:T(128)S(1)}, f32[4,1024]{1,0:T(4,128)S(1)}) fusion(bf16[1024,1024]{1,0:T(8,128)(2,1)} %get-tuple-element.967, f32[4,1024]{1,0:T(4,128)S(1)} %get-tuple-element.951, f32[1024]{0:T(1024)S(1)} %get-tuple-element.966, pred[4]{0:T(512)(128)(4,1)S(1)} %compare_bitcast_fusion.13, f32[8,4,1024]{2,1,0:T(4,128)S(1)} %get-tuple-element.964, ...), kind=kOutput, calls=%fused_computation.70.clone.1 | convolution fusion | flops 8404988 | bytes 2150424 | tf_op jit(solution)/shard_map/while/body/eval_jaxpr/dot_general | solution.py:44
  121.1 6.2 %while.83 = (s32[]{:T(128)}, f32[4,1024]{1,0:T(4,128)S(1)}, f32[8,4,1024]{2,0,1:T(8,128)S(1)}, s32[8,4]{1,0:T(8,128)S(1)}, f32[8,4,1024]{2,1,0:T(4,128)S(1)}, /*...) while((s32[]{:T(128)}, f32[4,1024]{1,0:T(4,128)S(1)}, ...), condition=%wide.region_20.21_spmd, body=%wide.region_18.20_spmd.sunk | while | flops 8409091 | bytes 2244781 | solution.py:66
  121.1 0.5 fusion.74
  127.4 0.7 copy.47
  128.1 1.1 reshape.120
  129.2 10.6 %all_to_all.36 = bf16[2,2,8192]{2,1,0:T(2,128)(2,1)S(1)} all-to-all(bf16[2,2,8192]{2,1,0:T(2,128)(2,1)S(1)} %reshape.120), channel_id=1, replica_groups=mesh['tm'=256,'state'=2] {'state'}, dimensions={0} | all-to-all | bytes 131072 | tf_op jit(solution)/shard_map/all_to_all | solution.py:113
  139.8 1.2 reshape.121
  141.0 1.2 copy.48
  142.2 0.7 copy.49
  (196 shorter events, 15.4 us)
Async XLA Ops:
  7.2 10.8 %copy-start = (s32[4,16]{1,0:T(4,128)S(1)}, s32[4,16]{1,0:T(4,128)}, u32[]{:S(2)}) copy-start(s32[4,16]{1,0:T(4,128)} %param.23) | copy-start | bytes 772
  7.2 1.6 %copy-start.4 = (bf16[512]{0:T(512)(128)(2,1)S(1)}, bf16[512]{0:T(512)(128)(2,1)}, u32[]{:S(2)}) copy-start(bf16[512]{0:T(512)(128)(2,1)} %param.22) | copy-start | bytes 3076
  7.2 23.9 %all-gather.2.cloned.1.call-start = ((), (), s32[]{:S(2)}) async-start(), calls=%async_computation.2 | async-start | bytes 3170304 | tf_op jit(solution)/shard_map/all_gather | solution.py:13
  8.8 1.6 %copy-start.1 = (f32[512,512]{1,0:T(8,128)S(1)}, f32[512,512]{1,0:T(8,128)}, u32[]{:S(2)}) copy-start(f32[512,512]{1,0:T(8,128)} %param.20) | copy-start | bytes 3145732
  8.8 1.9 %copy-start.2 = (f32[512,512]{1,0:T(8,128)S(1)}, f32[512,512]{1,0:T(8,128)}, u32[]{:S(2)}) copy-start(f32[512,512]{1,0:T(8,128)} %param.19) | copy-start | bytes 3145732
  9.9 1.1 copy-start.3
  14.0 5.2 %all-to-all-start = ((f32[4,16,512]{2,0,1:T(4,128)}), f32[4,16,512]{2,0,1:T(4,128)S(1)}, u32[]{:S(2)}, u32[]{:S(2)}) async-start(f32[4,16,512]{2,0,1:T(4,128)} %copy.38), calls=%async_computation | async-start | bytes 262144 | tf_op jit(solution)/shard_map/all_to_all | solution.py:108
  58.8 9.9 %collective-permute-start = (f32[4,1024]{1,0:T(4,128)S(1)}, f32[4,1024]{1,0:T(4,128)S(1)}, u32[]{:S(2)}, u32[]{:S(2)}) collective-permute-start(f32[4,1024]{1,0:T(4,128)S(1)} %get-tuple-element.437), channel_id=1, source_target_pairs={{0,1},{1,2},{2,3},{3,4},{4,5},{5,6},{6,7},{7,8},{8,9},{9,10},{10,1... | collective-permute-start | bytes 49160 | tf_op jit(solution)/shard_map/ppermute | solution.py:24
  66.8 23.2 %collective-permute-start.2 = (f32[4,1024]{1,0:T(4,128)S(1)}, f32[4,1024]{1,0:T(4,128)S(1)}, u32[]{:S(2)}, u32[]{:S(2)}) collective-permute-start(f32[4,1024]{1,0:T(4,128)S(1)} %get-tuple-element.440), channel_id=1, source_target_pairs={{1,0},{2,1},{3,2},{4,3},{5,4},{6,5},{7,6},{8,7},{9,8},{10,9},{11,1... | collective-permute-start | bytes 49160 | tf_op jit(solution)/shard_map/ppermute | solution.py:24
  86.3 14.7 %collective-permute-start.1 = (f32[4,1024]{1,0:T(4,128)S(1)}, f32[4,1024]{1,0:T(4,128)S(1)}, u32[]{:S(2)}, u32[]{:S(2)}) collective-permute-start(f32[4,1024]{1,0:T(4,128)S(1)} %get-tuple-element.438), channel_id=1, source_target_pairs={{0,1},{1,2},{2,3},{3,4},{4,5},{5,6},{6,7},{7,8},{8,9},{9,10},{10,1... | collective-permute-start | bytes 49160 | tf_op jit(solution)/shard_map/ppermute | solution.py:24
  94.7 26.3 %collective-permute-start.3 = (f32[4,1024]{1,0:T(4,128)S(1)}, f32[4,1024]{1,0:T(4,128)S(1)}, u32[]{:S(2)}, u32[]{:S(2)}) collective-permute-start(f32[4,1024]{1,0:T(4,128)S(1)} %get-tuple-element.441), channel_id=1, source_target_pairs={{1,0},{2,1},{3,2},{4,3},{5,4},{6,5},{7,6},{8,7},{9,8},{10,9},{11,1... | collective-permute-start | bytes 49160 | tf_op jit(solution)/shard_map/ppermute | solution.py:24
Sparse Core Ops, SparseCore 0:
  10.1 20.9 all-gather.1
where the time goes:
time: 151 us; the launch traced here: 150 us
  matrix products  64.5 us (43%)
  starting transfers between devices  19.1 us (13%)
  local copies, waits for them, and re-layouts  18.4 us (12%)
  between operations  14.3 us (9%)
  waiting for transfers between devices  12.7 us (8%)
  blocking collectives  10.6 us (7%)
  other arithmetic  9.28 us (6%)
    dot_general x24, matrix products, forward_step(): jnp.dot(alpha_prev.astype(jnp.bfloat16), trans, preferred_element_type=jn...  50.3 us
    ppermute x4, starting transfers between devices, passed_along(): return lax.ppermute(block, axis, route)  15 us
    dot_general x24, matrix products, backward_step(): jnp.dot((emit_row * beta_next).astype(jnp.bfloat16), trans_back, preferre...  11.9 us
    all_gather x1, waiting for transfers between devices, in_one_piece(): lax.all_gather(both, axis, axis=dim, tiled=True)  11.7 us
    all_to_all x1, blocking collectives, per_device(): lax.all_to_all(posterior, 'state', split_axis=2, concat_axis=1, tiled=True)  10.6 us
    unnamed x15, local copies, waits for them, and re-layouts  8.69 us
    all_to_all x1, starting transfers between devices, per_device(): lax.all_to_all(scores, 'state', split_axis=1, concat_axis=2, tiled=True)  4.04 us
    transpose x1, local copies, waits for them, and re-layouts, per_device(): trans_back = trans.T  3.51 us
  transfers between devices with their start and end apart: 6, of which 2 were waited for; matrix products, arithmetic and copies ran while one was open for 34% of the time, Pallas kernels for 0%

commit v1 on v0

--- a/solution.py
+++ b/solution.py
@@ -110,7 +110,12 @@
     posterior, evidence = run_chain(
         my_scores, my_flags, trans, trans_back, prior_dist, relay_step, SPAN * group
     )
-    posteriors = lax.all_to_all(posterior, "state", split_axis=2, concat_axis=1, tiled=True)
+    posteriors = jnp.concatenate(
+        lax.all_to_all(
+            jnp.stack(jnp.split(posterior, lax.axis_size("state"), axis=2)), "state", 0, 0
+        ),
+        axis=1,
+    )
     return (posteriors, evidence)
 
 

time: 151 us -> 144 us (0.954)
  local copies, waits for them, and re-layouts: 18.4 us -> 12.5 us
    dynamic_update_slice x40 -> x16, local copies, waits for them, and re-layouts: 2.8 us -> 0.4 us  [run_block(): lax.scan(forward_step, alpha_in, (emission_t, reset_t))]
    unnamed x15 -> x13, local copies, waits for them, and re-layouts: 8.69 us -> 6.35 us
where the time goes in v1:
time: 144 us; the launch traced here: 143 us
  matrix products  64.4 us (45%)
  starting transfers between devices  19.1 us (13%)
  between operations  14.2 us (10%)
  waiting for transfers between devices  12.7 us (9%)
  local copies, waits for them, and re-layouts  12.5 us (9%)
  blocking collectives  10.6 us (7%)
  other arithmetic  8.84 us (6%)
    dot_general x24, matrix products, forward_step(): jnp.dot(alpha_prev.astype(jnp.bfloat16), trans, preferred_element_type=jn...  50.3 us
    ppermute x4, starting transfers between devices, passed_along(): return lax.ppermute(block, axis, route)  15 us
    dot_general x24, matrix products, backward_step(): jnp.dot((emit_row * beta_next).astype(jnp.bfloat16), trans_back, preferre...  11.9 us
    all_gather x1, waiting for transfers between devices, in_one_piece(): lax.all_gather(both, axis, axis=dim, tiled=True)  11.7 us
    all_to_all x1, blocking collectives, per_device(): lax.all_to_all(jnp.stack(jnp.split(posterior, lax.axis_size('state'), axi...  10.6 us
    unnamed x13, local copies, waits for them, and re-layouts  6.35 us
    all_to_all x1, starting transfers between devices, per_device(): lax.all_to_all(scores, 'state', split_axis=1, concat_axis=2, tiled=True)  4.04 us
    transpose x1, local copies, waits for them, and re-layouts, per_device(): trans_back = trans.T  3.45 us
  transfers between devices with their start and end apart: 6, of which 2 were waited for; matrix products, arithmetic and copies ran while one was open for 34% of the time, Pallas kernels for 0%

profile of v1, /device:TPU:257, one launch (start us, length us, event | category | flops | bytes accessed | tf_op | source)
XLA Modules:
  0.0 143.0 jit_solution(8086318603902848213)
XLA Ops:
  7.2 1.5 %copy.19 = bf16[512,1024]{0,1:T(8,128)(2,1)S(1)} copy(bf16[512,1024]{1,0:T(8,128)(2,1)} %param.21) | data formatting | bytes 2097152 | tf_op args[3]
  8.8 1.1 pad_maximum_fusion
  11.0 1.1 fusion.30
  12.0 1.2 fusion.27
  13.2 0.7 copy.16
  14.0 4.0 %all-to-all-start = ((f32[4,16,512]{2,0,1:T(4,128)}), f32[4,16,512]{2,0,1:T(4,128)S(1)}, u32[]{:S(2)}, u32[]{:S(2)}) async-start(f32[4,16,512]{2,0,1:T(4,128)} %copy.16), calls=%async_computation | async-start | bytes 262144 | tf_op jit(solution)/shard_map/all_to_all | solution.py:108
  18.2 0.9 all-to-all-done
  19.4 11.7 %all-gather.2.cloned.1.call-done = bf16[1024,1025]{0,1:T(8,128)(2,1)} async-done(((bf16[512,1025]{0,1:T(8,128)(2,1)}), bf16[1024,1025]{0,1:T(8,128)(2,1)}) %all-gather.2.cloned.1.call-update) | async-done | bytes 2099216 | tf_op jit(solution)/shard_map/all_gather | solution.py:13
  31.1 3.4 %slice_bitcast_fusion.2 = (bf16[1024,1024]{1,0:T(8,128)(2,1)S(1)}, bf16[1024,1024]{0,1:T(8,128)(2,1)}) fusion(bf16[1024,1025]{0,1:T(8,128)(2,1)} %all-gather.2.cloned.1.call-done), kind=kLoop, calls=%fused_computation.76 | loop fusion | bytes 6291456 | tf_op jit(solution)/shard_map/transpose | solution.py:90
  34.5 3.9 %copy.20 = bf16[1024,1024]{1,0:T(8,128)(2,1)} copy(bf16[1024,1024]{0,1:T(8,128)(2,1)} %get-tuple-element.610) | data formatting | bytes 4194304
  38.5 1.4 fusion.37
  39.8 1.3 fusion.36
  41.1 17.6 %while.84 = (s32[]{:T(128)}, bf16[4,1024]{1,0:T(4,128)(2,1)S(1)}, f32[8,4,1024]{2,1,0:T(4,128)S(1)}, s32[8,4]{1,0:T(8,128)S(1)}, f32[1024]{0:T(1024)S(1)}, /*index=5*/bf16[1024,1024]{1,0:T(8,128)(2,1)}, s32[]{:T(128)}, s32[]{:T(128)}) while((s32[]{:T(128)}, bf16[4,1024]{1,0:T(4,128)(2,1)S(1)}, f32[8,4,1024]{2,1,0:T(4,128)S(1)}, ...), condition=%wide.region_5.6_spmd.clone, body=%wide.region_3.5_spmd.clone.sunk | while | flops 8413187 | bytes 2166943 | solution.py:53
  41.2 2.1 %fusion.79 = (f32[4]{0:T(128)S(1)}, f32[4,1024]{1,0:T(4,128)S(1)}) fusion(bf16[1024,1024]{1,0:T(8,128)(2,1)} %get-tuple-element.886, bf16[4,1024]{1,0:T(4,128)(2,1)S(1)} %get-tuple-element.874, pred[]{:T(512)S(6)} %compare.6, f32[1024]{0:T(1024)S(1)} %get-tuple-element.885, pred[4]{0:T(512)(128)(4,1)S(1)} %compare_bitcast_fusion.16, ...), kind=kOutput, calls=%fused_computation.80.clone.1 | convolution fusion | flops 8404988 | bytes 2142233 | tf_op jit(solution)/shard_map/while/body/eval_jaxpr/dot_general | solution.py:44
  43.4 2.1 %fusion.79 = (f32[4]{0:T(128)S(1)}, f32[4,1024]{1,0:T(4,128)S(1)}) fusion(bf16[1024,1024]{1,0:T(8,128)(2,1)} %get-tuple-element.886, bf16[4,1024]{1,0:T(4,128)(2,1)S(1)} %get-tuple-element.874, pred[]{:T(512)S(6)} %compare.6, f32[1024]{0:T(1024)S(1)} %get-tuple-element.885, pred[4]{0:T(512)(128)(4,1)S(1)} %compare_bitcast_fusion.16, ...), kind=kOutput, calls=%fused_computation.80.clone.1 | convolution fusion | flops 8404988 | bytes 2142233 | tf_op jit(solution)/shard_map/while/body/eval_jaxpr/dot_general | solution.py:44
  45.6 2.1 %fusion.79 = (f32[4]{0:T(128)S(1)}, f32[4,1024]{1,0:T(4,128)S(1)}) fusion(bf16[1024,1024]{1,0:T(8,128)(2,1)} %get-tuple-element.886, bf16[4,1024]{1,0:T(4,128)(2,1)S(1)} %get-tuple-element.874, pred[]{:T(512)S(6)} %compare.6, f32[1024]{0:T(1024)S(1)} %get-tuple-element.885, pred[4]{0:T(512)(128)(4,1)S(1)} %compare_bitcast_fusion.16, ...), kind=kOutput, calls=%fused_computation.80.clone.1 | convolution fusion | flops 8404988 | bytes 2142233 | tf_op jit(solution)/shard_map/while/body/eval_jaxpr/dot_general | solution.py:44
  47.8 2.1 %fusion.79 = (f32[4]{0:T(128)S(1)}, f32[4,1024]{1,0:T(4,128)S(1)}) fusion(bf16[1024,1024]{1,0:T(8,128)(2,1)} %get-tuple-element.886, bf16[4,1024]{1,0:T(4,128)(2,1)S(1)} %get-tuple-element.874, pred[]{:T(512)S(6)} %compare.6, f32[1024]{0:T(1024)S(1)} %get-tuple-element.885, pred[4]{0:T(512)(128)(4,1)S(1)} %compare_bitcast_fusion.16, ...), kind=kOutput, calls=%fused_computation.80.clone.1 | convolution fusion | flops 8404988 | bytes 2142233 | tf_op jit(solution)/shard_map/while/body/eval_jaxpr/dot_general | solution.py:44
  50.0 2.1 %fusion.79 = (f32[4]{0:T(128)S(1)}, f32[4,1024]{1,0:T(4,128)S(1)}) fusion(bf16[1024,1024]{1,0:T(8,128)(2,1)} %get-tuple-element.886, bf16[4,1024]{1,0:T(4,128)(2,1)S(1)} %get-tuple-element.874, pred[]{:T(512)S(6)} %compare.6, f32[1024]{0:T(1024)S(1)} %get-tuple-element.885, pred[4]{0:T(512)(128)(4,1)S(1)} %compare_bitcast_fusion.16, ...), kind=kOutput, calls=%fused_computation.80.clone.1 | convolution fusion | flops 8404988 | bytes 2142233 | tf_op jit(solution)/shard_map/while/body/eval_jaxpr/dot_general | solution.py:44
  52.2 2.1 %fusion.79 = (f32[4]{0:T(128)S(1)}, f32[4,1024]{1,0:T(4,128)S(1)}) fusion(bf16[1024,1024]{1,0:T(8,128)(2,1)} %get-tuple-element.886, bf16[4,1024]{1,0:T(4,128)(2,1)S(1)} %get-tuple-element.874, pred[]{:T(512)S(6)} %compare.6, f32[1024]{0:T(1024)S(1)} %get-tuple-element.885, pred[4]{0:T(512)(128)(4,1)S(1)} %compare_bitcast_fusion.16, ...), kind=kOutput, calls=%fused_computation.80.clone.1 | convolution fusion | flops 8404988 | bytes 2142233 | tf_op jit(solution)/shard_map/while/body/eval_jaxpr/dot_general | solution.py:44
  54.4 2.1 %fusion.79 = (f32[4]{0:T(128)S(1)}, f32[4,1024]{1,0:T(4,128)S(1)}) fusion(bf16[1024,1024]{1,0:T(8,128)(2,1)} %get-tuple-element.886, bf16[4,1024]{1,0:T(4,128)(2,1)S(1)} %get-tuple-element.874, pred[]{:T(512)S(6)} %compare.6, f32[1024]{0:T(1024)S(1)} %get-tuple-element.885, pred[4]{0:T(512)(128)(4,1)S(1)} %compare_bitcast_fusion.16, ...), kind=kOutput, calls=%fused_computation.80.clone.1 | convolution fusion | flops 8404988 | bytes 2142233 | tf_op jit(solution)/shard_map/while/body/eval_jaxpr/dot_general | solution.py:44
  56.6 2.1 %fusion.79 = (f32[4]{0:T(128)S(1)}, f32[4,1024]{1,0:T(4,128)S(1)}) fusion(bf16[1024,1024]{1,0:T(8,128)(2,1)} %get-tuple-element.886, bf16[4,1024]{1,0:T(4,128)(2,1)S(1)} %get-tuple-element.874, pred[]{:T(512)S(6)} %compare.6, f32[1024]{0:T(1024)S(1)} %get-tuple-element.885, pred[4]{0:T(512)(128)(4,1)S(1)} %compare_bitcast_fusion.16, ...), kind=kOutput, calls=%fused_computation.80.clone.1 | convolution fusion | flops 8404988 | bytes 2142233 | tf_op jit(solution)/shard_map/while/body/eval_jaxpr/dot_general | solution.py:44
  58.7 3.2 %collective-permute-start = (bf16[4,1024]{1,0:T(4,128)(2,1)S(1)}, bf16[4,1024]{1,0:T(4,128)(2,1)S(1)}, u32[]{:S(2)}, u32[]{:S(2)}) collective-permute-start(bf16[4,1024]{1,0:T(4,128)(2,1)S(1)} %get-tuple-element.437), channel_id=1, source_target_pairs={{0,1},{1,2},{2,3},{3,4},{4,5},{5,6},{6,7},{7,8},{8,9},{9,10},{10,1... | collective-permute-start | bytes 24584 | tf_op jit(solution)/shard_map/ppermute | solution.py:24
  61.9 4.8 %while.85 = (s32[]{:T(128)}, f32[4,1024]{1,0:T(4,128)S(1)}, s32[8,4]{1,0:T(8,128)S(1)}, f32[8,4,1024]{2,1,0:T(4,128)S(1)}, bf16[1024,1024]{1,0:T(8,128)(2,1)S(1)}, /*index=5*/s32[]{:T(128)}, s32[]{:T(128)}, s32[]{:T(128)}) while((s32[]{:T(128)}, f32[4,1024]{1,0:T(4,128)S(1)}, s32[8,4]{1,0:T(8,128)S(1)}, ...), condition=%wide.region_14.15_spmd.clone, body=%wide.region_12.14_spmd.clone.sunk | while | flops 8413188 | bytes 2179243 | solution.py:66
  62.0 0.5 fusion.81
  62.6 0.5 fusion.81
  63.1 0.5 fusion.81
  63.7 0.5 fusion.81
  64.3 0.5 fusion.81
  64.9 0.5 fusion.81
  65.5 0.5 fusion.81
  66.1 0.5 fusion.81
  66.7 1.9 %collective-permute-start.2 = (f32[4,1024]{1,0:T(4,128)S(1)}, f32[4,1024]{1,0:T(4,128)S(1)}, u32[]{:S(2)}, u32[]{:S(2)}) collective-permute-start(f32[4,1024]{1,0:T(4,128)S(1)} %get-tuple-element.440), channel_id=1, source_target_pairs={{1,0},{2,1},{3,2},{4,3},{5,4},{6,5},{7,6},{8,7},{9,8},{10,9},{11,1... | collective-permute-start | bytes 49160 | tf_op jit(solution)/shard_map/ppermute | solution.py:24
  68.6 17.6 %while.80 = (s32[]{:T(128)}, bf16[4,1024]{1,0:T(4,128)(2,1)S(1)}, f32[8,4,1024]{2,1,0:T(4,128)S(1)}, s32[8,4]{1,0:T(8,128)S(1)}, f32[1024]{0:T(1024)S(1)}, /*index=5*/bf16[1024,1024]{1,0:T(8,128)(2,1)}, s32[]{:T(128)}) while((s32[]{:T(128)}, bf16[4,1024]{1,0:T(4,128)(2,1)S(1)}, f32[8,4,1024]{2,1,0:T(4,128)S(1)}, s32[8,4]{1,0:T(8,128)S(1)}, ...), condition=%wide.region_8.9_spmd, body=%wide.region_6.8_spmd.sunk | while | flops 8409090 | bytes 2166925 | solution.py:53
  68.7 2.1 %fusion.70 = (f32[4]{0:T(128)S(1)}, f32[4,1024]{1,0:T(4,128)S(1)}) fusion(bf16[1024,1024]{1,0:T(8,128)(2,1)} %get-tuple-element.908, bf16[4,1024]{1,0:T(4,128)(2,1)S(1)} %get-tuple-element.897, f32[1024]{0:T(1024)S(1)} %get-tuple-element.907, pred[4]{0:T(512)(128)(4,1)S(1)} %compare_bitcast_fusion.12, f32[8,4,1024]{2,1,0:T(4,128)S(1)} %get-tuple-element.905, ...), kind=kOutput, calls=%fused_computation.77.clone.1 | convolution fusion | flops 8400892 | bytes 2142232 | tf_op jit(solution)/shard_map/while/body/eval_jaxpr/dot_general | solution.py:44
  70.9 2.1 %fusion.70 = (f32[4]{0:T(128)S(1)}, f32[4,1024]{1,0:T(4,128)S(1)}) fusion(bf16[1024,1024]{1,0:T(8,128)(2,1)} %get-tuple-element.908, bf16[4,1024]{1,0:T(4,128)(2,1)S(1)} %get-tuple-element.897, f32[1024]{0:T(1024)S(1)} %get-tuple-element.907, pred[4]{0:T(512)(128)(4,1)S(1)} %compare_bitcast_fusion.12, f32[8,4,1024]{2,1,0:T(4,128)S(1)} %get-tuple-element.905, ...), kind=kOutput, calls=%fused_computation.77.clone.1 | convolution fusion | flops 8400892 | bytes 2142232 | tf_op jit(solution)/shard_map/while/body/eval_jaxpr/dot_general | solution.py:44
  73.1 2.1 %fusion.70 = (f32[4]{0:T(128)S(1)}, f32[4,1024]{1,0:T(4,128)S(1)}) fusion(bf16[1024,1024]{1,0:T(8,128)(2,1)} %get-tuple-element.908, bf16[4,1024]{1,0:T(4,128)(2,1)S(1)} %get-tuple-element.897, f32[1024]{0:T(1024)S(1)} %get-tuple-element.907, pred[4]{0:T(512)(128)(4,1)S(1)} %compare_bitcast_fusion.12, f32[8,4,1024]{2,1,0:T(4,128)S(1)} %get-tuple-element.905, ...), kind=kOutput, calls=%fused_computation.77.clone.1 | convolution fusion | flops 8400892 | bytes 2142232 | tf_op jit(solution)/shard_map/while/body/eval_jaxpr/dot_general | solution.py:44
  75.3 2.1 %fusion.70 = (f32[4]{0:T(128)S(1)}, f32[4,1024]{1,0:T(4,128)S(1)}) fusion(bf16[1024,1024]{1,0:T(8,128)(2,1)} %get-tuple-element.908, bf16[4,1024]{1,0:T(4,128)(2,1)S(1)} %get-tuple-element.897, f32[1024]{0:T(1024)S(1)} %get-tuple-element.907, pred[4]{0:T(512)(128)(4,1)S(1)} %compare_bitcast_fusion.12, f32[8,4,1024]{2,1,0:T(4,128)S(1)} %get-tuple-element.905, ...), kind=kOutput, calls=%fused_computation.77.clone.1 | convolution fusion | flops 8400892 | bytes 2142232 | tf_op jit(solution)/shard_map/while/body/eval_jaxpr/dot_general | solution.py:44
  77.5 2.1 %fusion.70 = (f32[4]{0:T(128)S(1)}, f32[4,1024]{1,0:T(4,128)S(1)}) fusion(bf16[1024,1024]{1,0:T(8,128)(2,1)} %get-tuple-element.908, bf16[4,1024]{1,0:T(4,128)(2,1)S(1)} %get-tuple-element.897, f32[1024]{0:T(1024)S(1)} %get-tuple-element.907, pred[4]{0:T(512)(128)(4,1)S(1)} %compare_bitcast_fusion.12, f32[8,4,1024]{2,1,0:T(4,128)S(1)} %get-tuple-element.905, ...), kind=kOutput, calls=%fused_computation.77.clone.1 | convolution fusion | flops 8400892 | bytes 2142232 | tf_op jit(solution)/shard_map/while/body/eval_jaxpr/dot_general | solution.py:44
  79.7 2.1 %fusion.70 = (f32[4]{0:T(128)S(1)}, f32[4,1024]{1,0:T(4,128)S(1)}) fusion(bf16[1024,1024]{1,0:T(8,128)(2,1)} %get-tuple-element.908, bf16[4,1024]{1,0:T(4,128)(2,1)S(1)} %get-tuple-element.897, f32[1024]{0:T(1024)S(1)} %get-tuple-element.907, pred[4]{0:T(512)(128)(4,1)S(1)} %compare_bitcast_fusion.12, f32[8,4,1024]{2,1,0:T(4,128)S(1)} %get-tuple-element.905, ...), kind=kOutput, calls=%fused_computation.77.clone.1 | convolution fusion | flops 8400892 | bytes 2142232 | tf_op jit(solution)/shard_map/while/body/eval_jaxpr/dot_general | solution.py:44
  81.9 2.1 %fusion.70 = (f32[4]{0:T(128)S(1)}, f32[4,1024]{1,0:T(4,128)S(1)}) fusion(bf16[1024,1024]{1,0:T(8,128)(2,1)} %get-tuple-element.908, bf16[4,1024]{1,0:T(4,128)(2,1)S(1)} %get-tuple-element.897, f32[1024]{0:T(1024)S(1)} %get-tuple-element.907, pred[4]{0:T(512)(128)(4,1)S(1)} %compare_bitcast_fusion.12, f32[8,4,1024]{2,1,0:T(4,128)S(1)} %get-tuple-element.905, ...), kind=kOutput, calls=%fused_computation.77.clone.1 | convolution fusion | flops 8400892 | bytes 2142232 | tf_op jit(solution)/shard_map/while/body/eval_jaxpr/dot_general | solution.py:44
  84.0 2.1 %fusion.70 = (f32[4]{0:T(128)S(1)}, f32[4,1024]{1,0:T(4,128)S(1)}) fusion(bf16[1024,1024]{1,0:T(8,128)(2,1)} %get-tuple-element.908, bf16[4,1024]{1,0:T(4,128)(2,1)S(1)} %get-tuple-element.897, f32[1024]{0:T(1024)S(1)} %get-tuple-element.907, pred[4]{0:T(512)(128)(4,1)S(1)} %compare_bitcast_fusion.12, f32[8,4,1024]{2,1,0:T(4,128)S(1)} %get-tuple-element.905, ...), kind=kOutput, calls=%fused_computation.77.clone.1 | convolution fusion | flops 8400892 | bytes 2142232 | tf_op jit(solution)/shard_map/while/body/eval_jaxpr/dot_general | solution.py:44
  86.2 3.6 %collective-permute-start.1 = (bf16[4,1024]{1,0:T(4,128)(2,1)S(1)}, bf16[4,1024]{1,0:T(4,128)(2,1)S(1)}, u32[]{:S(2)}, u32[]{:S(2)}) collective-permute-start(bf16[4,1024]{1,0:T(4,128)(2,1)S(1)} %get-tuple-element.438), channel_id=1, source_target_pairs={{0,1},{1,2},{2,3},{3,4},{4,5},{5,6},{6,7},{7,8},{8,9},{9,10},{10,1... | collective-permute-start | bytes 24584 | tf_op jit(solution)/shard_map/ppermute | solution.py:24
  89.9 4.8 %while.82 = (s32[]{:T(128)}, f32[4,1024]{1,0:T(4,128)S(1)}, s32[8,4]{1,0:T(8,128)S(1)}, f32[8,4,1024]{2,1,0:T(4,128)S(1)}, bf16[1024,1024]{1,0:T(8,128)(2,1)S(1)}, /*index=5*/s32[]{:T(128)}, s32[]{:T(128)}) while((s32[]{:T(128)}, f32[4,1024]{1,0:T(4,128)S(1)}, s32[8,4]{1,0:T(8,128)S(1)}, f32[8,4,1024]{2,1,0:T(4,128)S(1)}, ...), condition=%wide.region_17.18_spmd, body=%wide.region_15.17_spmd.sunk | while | flops 8409091 | bytes 2179225 | solution.py:66
  89.9 0.5 fusion.75
  90.5 0.5 fusion.75
  91.1 0.5 fusion.75
  91.7 0.5 fusion.75
  92.3 0.5 fusion.75
  92.9 0.5 fusion.75
  94.1 0.5 fusion.75
  94.7 6.3 %collective-permute-start.3 = (f32[4,1024]{1,0:T(4,128)S(1)}, f32[4,1024]{1,0:T(4,128)S(1)}, u32[]{:S(2)}, u32[]{:S(2)}) collective-permute-start(f32[4,1024]{1,0:T(4,128)S(1)} %get-tuple-element.441), channel_id=1, source_target_pairs={{1,0},{2,1},{3,2},{4,3},{5,4},{6,5},{7,6},{8,7},{9,8},{10,9},{11,1... | collective-permute-start | bytes 49160 | tf_op jit(solution)/shard_map/ppermute | solution.py:24
  101.0 18.1 %while.81 = (s32[]{:T(128)}, bf16[4,1024]{1,0:T(4,128)(2,1)S(1)}, f32[8,4,1024]{2,1,0:T(4,128)S(1)}, f32[8,4]{1,0:T(8,128)S(1)}, f32[8,4,1024]{2,1,0:T(4,128)S(1...) while((s32[]{:T(128)}, bf16[4,1024]{1,0:T(4,128)(2,1)S(1)}, ...), condition=%wide.region_11.12_spmd, body=%wide.region_9.11_spmd.sunk | while | flops 8409090 | bytes 2183901 | solution.py:53
  101.0 2.1 %fusion.73 = (f32[4]{0:T(128)S(1)}, f32[4,1024]{1,0:T(4,128)S(1)}) fusion(bf16[1024,1024]{1,0:T(8,128)(2,1)} %get-tuple-element.937, bf16[4,1024]{1,0:T(4,128)(2,1)S(1)} %get-tuple-element.921, f32[1024]{0:T(1024)S(1)} %get-tuple-element.936, pred[4]{0:T(512)(128)(4,1)S(1)} %compare_bitcast_fusion.13, f32[8,4,1024]{2,1,0:T(4,128)S(1)} %get-tuple-element.934, ...), kind=kOutput, calls=%fused_computation.82.clone.1 | convolution fusion | flops 8400892 | bytes 2142232 | tf_op jit(solution)/shard_map/while/body/eval_jaxpr/dot_general | solution.py:44
  103.3 2.1 %fusion.73 = (f32[4]{0:T(128)S(1)}, f32[4,1024]{1,0:T(4,128)S(1)}) fusion(bf16[1024,1024]{1,0:T(8,128)(2,1)} %get-tuple-element.937, bf16[4,1024]{1,0:T(4,128)(2,1)S(1)} %get-tuple-element.921, f32[1024]{0:T(1024)S(1)} %get-tuple-element.936, pred[4]{0:T(512)(128)(4,1)S(1)} %compare_bitcast_fusion.13, f32[8,4,1024]{2,1,0:T(4,128)S(1)} %get-tuple-element.934, ...), kind=kOutput, calls=%fused_computation.82.clone.1 | convolution fusion | flops 8400892 | bytes 2142232 | tf_op jit(solution)/shard_map/while/body/eval_jaxpr/dot_general | solution.py:44
  105.5 2.1 %fusion.73 = (f32[4]{0:T(128)S(1)}, f32[4,1024]{1,0:T(4,128)S(1)}) fusion(bf16[1024,1024]{1,0:T(8,128)(2,1)} %get-tuple-element.937, bf16[4,1024]{1,0:T(4,128)(2,1)S(1)} %get-tuple-element.921, f32[1024]{0:T(1024)S(1)} %get-tuple-element.936, pred[4]{0:T(512)(128)(4,1)S(1)} %compare_bitcast_fusion.13, f32[8,4,1024]{2,1,0:T(4,128)S(1)} %get-tuple-element.934, ...), kind=kOutput, calls=%fused_computation.82.clone.1 | convolution fusion | flops 8400892 | bytes 2142232 | tf_op jit(solution)/shard_map/while/body/eval_jaxpr/dot_general | solution.py:44
  107.8 2.1 %fusion.73 = (f32[4]{0:T(128)S(1)}, f32[4,1024]{1,0:T(4,128)S(1)}) fusion(bf16[1024,1024]{1,0:T(8,128)(2,1)} %get-tuple-element.937, bf16[4,1024]{1,0:T(4,128)(2,1)S(1)} %get-tuple-element.921, f32[1024]{0:T(1024)S(1)} %get-tuple-element.936, pred[4]{0:T(512)(128)(4,1)S(1)} %compare_bitcast_fusion.13, f32[8,4,1024]{2,1,0:T(4,128)S(1)} %get-tuple-element.934, ...), kind=kOutput, calls=%fused_computation.82.clone.1 | convolution fusion | flops 8400892 | bytes 2142232 | tf_op jit(solution)/shard_map/while/body/eval_jaxpr/dot_general | solution.py:44
  110.1 2.1 %fusion.73 = (f32[4]{0:T(128)S(1)}, f32[4,1024]{1,0:T(4,128)S(1)}) fusion(bf16[1024,1024]{1,0:T(8,128)(2,1)} %get-tuple-element.937, bf16[4,1024]{1,0:T(4,128)(2,1)S(1)} %get-tuple-element.921, f32[1024]{0:T(1024)S(1)} %get-tuple-element.936, pred[4]{0:T(512)(128)(4,1)S(1)} %compare_bitcast_fusion.13, f32[8,4,1024]{2,1,0:T(4,128)S(1)} %get-tuple-element.934, ...), kind=kOutput, calls=%fused_computation.82.clone.1 | convolution fusion | flops 8400892 | bytes 2142232 | tf_op jit(solution)/shard_map/while/body/eval_jaxpr/dot_general | solution.py:44
  112.3 2.1 %fusion.73 = (f32[4]{0:T(128)S(1)}, f32[4,1024]{1,0:T(4,128)S(1)}) fusion(bf16[1024,1024]{1,0:T(8,128)(2,1)} %get-tuple-element.937, bf16[4,1024]{1,0:T(4,128)(2,1)S(1)} %get-tuple-element.921, f32[1024]{0:T(1024)S(1)} %get-tuple-element.936, pred[4]{0:T(512)(128)(4,1)S(1)} %compare_bitcast_fusion.13, f32[8,4,1024]{2,1,0:T(4,128)S(1)} %get-tuple-element.934, ...), kind=kOutput, calls=%fused_computation.82.clone.1 | convolution fusion | flops 8400892 | bytes 2142232 | tf_op jit(solution)/shard_map/while/body/eval_jaxpr/dot_general | solution.py:44
  114.6 2.1 %fusion.73 = (f32[4]{0:T(128)S(1)}, f32[4,1024]{1,0:T(4,128)S(1)}) fusion(bf16[1024,1024]{1,0:T(8,128)(2,1)} %get-tuple-element.937, bf16[4,1024]{1,0:T(4,128)(2,1)S(1)} %get-tuple-element.921, f32[1024]{0:T(1024)S(1)} %get-tuple-element.936, pred[4]{0:T(512)(128)(4,1)S(1)} %compare_bitcast_fusion.13, f32[8,4,1024]{2,1,0:T(4,128)S(1)} %get-tuple-element.934, ...), kind=kOutput, calls=%fused_computation.82.clone.1 | convolution fusion | flops 8400892 | bytes 2142232 | tf_op jit(solution)/shard_map/while/body/eval_jaxpr/dot_general | solution.py:44
  116.8 2.1 %fusion.73 = (f32[4]{0:T(128)S(1)}, f32[4,1024]{1,0:T(4,128)S(1)}) fusion(bf16[1024,1024]{1,0:T(8,128)(2,1)} %get-tuple-element.937, bf16[4,1024]{1,0:T(4,128)(2,1)S(1)} %get-tuple-element.921, f32[1024]{0:T(1024)S(1)} %get-tuple-element.936, pred[4]{0:T(512)(128)(4,1)S(1)} %compare_bitcast_fusion.13, f32[8,4,1024]{2,1,0:T(4,128)S(1)} %get-tuple-element.934, ...), kind=kOutput, calls=%fused_computation.82.clone.1 | convolution fusion | flops 8400892 | bytes 2142232 | tf_op jit(solution)/shard_map/while/body/eval_jaxpr/dot_general | solution.py:44
  119.1 0.7 copy.24
  119.8 4.9 %while.83 = (s32[]{:T(128)}, f32[4,1024]{1,0:T(4,128)S(1)}, f32[8,4,1024]{2,1,0:T(4,128)S(1)}, s32[8,4]{1,0:T(8,128)S(1)}, f32[8,4,1024]{2,1,0:T(4,128)S(1)}, /*...) while((s32[]{:T(128)}, f32[4,1024]{1,0:T(4,128)S(1)}, f32[8,4,1024]{2,1,0:T(4,128)S(1)}, ...), condition=%wide.region_20.21_spmd, body=%wide.region_18.20_spmd.sunk | while | flops 8409091 | bytes 2212005 | solution.py:66
  124.9 10.6 %all_to_all.23 = bf16[2,4,8,512]{3,1,2,0:T(4,128)(2,1)S(1)} all-to-all(bf16[2,4,8,512]{3,1,2,0:T(4,128)(2,1)S(1)} %pad_maximum_fusion.1), channel_id=1, replica_groups=mesh['tm'=256,'state'=2] {'state'}, dimensions={0} | all-to-all | bytes 131072 | tf_op jit(solution)/shard_map/all_to_all | solution.py:114
  135.5 0.6 copy.28
  (163 shorter events, 11.1 us)
Async XLA Ops:
  7.2 10.8 %copy-start = (s32[4,16]{1,0:T(4,128)S(1)}, s32[4,16]{1,0:T(4,128)}, u32[]{:S(2)}) copy-start(s32[4,16]{1,0:T(4,128)} %param.23) | copy-start | bytes 772
  7.2 1.6 %copy-start.4 = (bf16[512]{0:T(512)(128)(2,1)S(1)}, bf16[512]{0:T(512)(128)(2,1)}, u32[]{:S(2)}) copy-start(bf16[512]{0:T(512)(128)(2,1)} %param.22) | copy-start | bytes 3076
  7.2 23.9 %all-gather.2.cloned.1.call-start = ((), (), s32[]{:S(2)}) async-start(), calls=%async_computation.2 | async-start | bytes 3170304 | tf_op jit(solution)/shard_map/all_gather | solution.py:13
  8.8 1.6 %copy-start.1 = (f32[512,512]{1,0:T(8,128)S(1)}, f32[512,512]{1,0:T(8,128)}, u32[]{:S(2)}) copy-start(f32[512,512]{1,0:T(8,128)} %param.20) | copy-start | bytes 3145732
  8.8 1.9 %copy-start.2 = (f32[512,512]{1,0:T(8,128)S(1)}, f32[512,512]{1,0:T(8,128)}, u32[]{:S(2)}) copy-start(f32[512,512]{1,0:T(8,128)} %param.19) | copy-start | bytes 3145732
  9.9 1.1 copy-start.3
  14.0 5.2 %all-to-all-start = ((f32[4,16,512]{2,0,1:T(4,128)}), f32[4,16,512]{2,0,1:T(4,128)S(1)}, u32[]{:S(2)}, u32[]{:S(2)}) async-start(f32[4,16,512]{2,0,1:T(4,128)} %copy.16), calls=%async_computation | async-start | bytes 262144 | tf_op jit(solution)/shard_map/all_to_all | solution.py:108
  58.7 9.9 %collective-permute-start = (bf16[4,1024]{1,0:T(4,128)(2,1)S(1)}, bf16[4,1024]{1,0:T(4,128)(2,1)S(1)}, u32[]{:S(2)}, u32[]{:S(2)}) collective-permute-start(bf16[4,1024]{1,0:T(4,128)(2,1)S(1)} %get-tuple-element.437), channel_id=1, source_target_pairs={{0,1},{1,2},{2,3},{3,4},{4,5},{5,6},{6,7},{7,8},{8,9},{9,10},{10,1... | collective-permute-start | bytes 24584 | tf_op jit(solution)/shard_map/ppermute | solution.py:24
  66.7 23.2 %collective-permute-start.2 = (f32[4,1024]{1,0:T(4,128)S(1)}, f32[4,1024]{1,0:T(4,128)S(1)}, u32[]{:S(2)}, u32[]{:S(2)}) collective-permute-start(f32[4,1024]{1,0:T(4,128)S(1)} %get-tuple-element.440), channel_id=1, source_target_pairs={{1,0},{2,1},{3,2},{4,3},{5,4},{6,5},{7,6},{8,7},{9,8},{10,9},{11,1... | collective-permute-start | bytes 49160 | tf_op jit(solution)/shard_map/ppermute | solution.py:24
  86.2 14.7 %collective-permute-start.1 = (bf16[4,1024]{1,0:T(4,128)(2,1)S(1)}, bf16[4,1024]{1,0:T(4,128)(2,1)S(1)}, u32[]{:S(2)}, u32[]{:S(2)}) collective-permute-start(bf16[4,1024]{1,0:T(4,128)(2,1)S(1)} %get-tuple-element.438), channel_id=1, source_target_pairs={{0,1},{1,2},{2,3},{3,4},{4,5},{5,6},{6,7},{7,8},{8,9},{9,10},{10,1... | collective-permute-start | bytes 24584 | tf_op jit(solution)/shard_map/ppermute | solution.py:24
  94.7 25.1 %collective-permute-start.3 = (f32[4,1024]{1,0:T(4,128)S(1)}, f32[4,1024]{1,0:T(4,128)S(1)}, u32[]{:S(2)}, u32[]{:S(2)}) collective-permute-start(f32[4,1024]{1,0:T(4,128)S(1)} %get-tuple-element.441), channel_id=1, source_target_pairs={{1,0},{2,1},{3,2},{4,3},{5,4},{6,5},{7,6},{8,7},{9,8},{10,9},{11,1... | collective-permute-start | bytes 49160 | tf_op jit(solution)/shard_map/ppermute | solution.py:24
Sparse Core Ops, SparseCore 0:
  10.1 20.9 all-gather.1
